TPU v7x, 256 devices: a whole 4x4x8 slice. The times are simulated.
256 devices in a mesh: seq: 32 (over z, y), tp: 8 (over x, core).
Axes of the slice: x: 4, y: 4, z: 8, core: 2. Of those that a mesh axis runs over, the one named last changes fastest.
Arguments:
- tokens: bfloat16 [16384, 4096], P('seq'), may hold values from -80 to 80
- norm_gain: float32 [4096], replicated, may hold values from 0.1 to 1.9
- query_weight: bfloat16 [4096, 4096], P(None, 'tp'), may hold values from -1 to 1
- key_weight: bfloat16 [4096, 1024], P(None, 'tp'), may hold values from -8 to 8
- value_weight: bfloat16 [4096, 1024], P(None, 'tp'), may hold values from -0.09375 to 0.09375
- out_weight: bfloat16 [4096, 4096], P(None, 'tp'), may hold values from -1 to 1
- segments: int32 [16384], replicated, may hold values from 0 to 2, never falling along the last dimension, each value on 1 to 8192 neighbouring positions
Outputs:
- attn_out: bfloat16 [16384, 4096], P('seq', 'tp')
All inputs are finite; a program needn't handle non-finite values.
Results may differ from a plain program's by a relative error of at most 0.013.
The roundings to bfloat16 on the way count: a program that leaves them out, or rounds other values in their place, can miss the bound.
Values may be sent and summed in bfloat16 or wider, within the bound.
A program may use at most 128 MiB of HBM per device.

v0:
```python
import math
import jax
import jax.numpy as jnp
from jax import lax
from jax.sharding import PartitionSpec as P

HEAD_DIM = 128
WINDOW = 4096


def shifted(value, axis, steps):
    count = lax.axis_size(axis)
    leading, last = (max(0, -steps), min(count, count - steps))
    return lax.ppermute(value, axis, [(source, source + steps) for source in range(leading, last)])


def rotate(vectors, positions):
    half_dim = vectors.shape[-1] // 2
    freqs = 10000.0 ** (-(jnp.arange(half_dim, dtype=jnp.float32) * 2.0 / vectors.shape[-1]))
    angles = positions[:, None] * freqs[None, :]
    cosine = jnp.cos(angles)[:, None, :]
    sine_part = jnp.sin(angles)[:, None, :]
    first = vectors[..., :half_dim]
    second = vectors[..., half_dim:]
    return jnp.concatenate(
        [first * cosine - second * sine_part, second * cosine + first * sine_part], axis=-1
    )


def project(normed, weight, positions):
    product = jnp.dot(normed, weight, preferred_element_type=jnp.float32)
    shaped = product.reshape(product.shape[0], -1, HEAD_DIM)
    return rotate(shaped, positions).astype(jnp.bfloat16)


def attend(queries, keys, values, allowed):
    block_rows, query_heads, head_size = queries.shape
    value_heads = keys.shape[1]
    grouped = queries.reshape(block_rows, value_heads, query_heads // value_heads, head_size)
    scores = jnp.einsum(
        "tkgd,skd->kgts", grouped, keys, preferred_element_type=jnp.float32
    ) / math.sqrt(head_size)
    scores = jnp.where(allowed[None, None], scores, jnp.float32(-1e30))
    peak = jnp.max(scores, axis=-1, keepdims=True)
    weights = jnp.exp(scores - peak)
    totals = jnp.sum(weights, axis=-1, keepdims=True)
    probabilities = (weights / totals).astype(jnp.bfloat16)
    attended = jnp.einsum(
        "kgts,skd->tkgd", probabilities, values, preferred_element_type=jnp.float32
    )
    return attended.reshape(block_rows, query_heads * head_size).astype(jnp.bfloat16)


def shards(tokens, norm_gain, query_weight, key_weight, value_weight, out_weight, segments):
    block_rows = tokens.shape[0]
    seq_index = lax.axis_index("seq")
    seq_count = lax.axis_size("seq")
    halo_blocks = min((WINDOW + block_rows - 2) // block_rows, seq_count - 1)
    widened = tokens.astype(jnp.float32)
    scale = lax.rsqrt(jnp.mean(widened * widened, axis=-1, keepdims=True) + 1e-05)
    normed = (widened * scale * norm_gain[None, :]).astype(jnp.bfloat16)
    first_token = seq_index * block_rows
    positions = (first_token + jnp.arange(block_rows, dtype=jnp.int32)).astype(jnp.float32)
    queries = project(normed, query_weight, positions)
    keys = project(normed, key_weight, positions)
    value_heads = keys.shape[1]
    values = jnp.dot(normed, value_weight, preferred_element_type=jnp.float32).astype(jnp.bfloat16)
    key_width = value_heads * HEAD_DIM
    key_value = jnp.concatenate([keys.reshape(block_rows, key_width), values], axis=1)
    front = halo_blocks * block_rows
    known_blocks = key_value
    gathered_count = 0
    while gathered_count < halo_blocks:
        taking = min(gathered_count + 1, halo_blocks - gathered_count)
        outgoing = known_blocks[known_blocks.shape[0] - taking * block_rows :]
        incoming = shifted(outgoing, "seq", gathered_count + 1)
        known_blocks = jnp.concatenate([incoming, known_blocks], axis=0)
        gathered_count = gathered_count + taking
    before = known_blocks[:front]
    window_rows = jnp.concatenate([before, key_value], axis=0)
    span = window_rows.shape[0]
    window_keys = window_rows[:, :key_width].reshape(span, value_heads, HEAD_DIM)
    window_values = window_rows[:, key_width:].reshape(span, value_heads, HEAD_DIM)
    padded_segments = jnp.concatenate([jnp.full((front,), -1, jnp.int32), segments], axis=0)
    start_index = seq_index * block_rows
    key_segments = lax.dynamic_slice_in_dim(padded_segments, start_index, span, 0)
    query_segments = lax.dynamic_slice_in_dim(segments, start_index, block_rows, 0)
    query_pos = start_index + jnp.arange(block_rows, dtype=jnp.int32)
    key_pos = start_index - front + jnp.arange(span, dtype=jnp.int32)
    distance = query_pos[:, None] - key_pos[None, :]
    allowed = (
        (distance >= 0) & (distance < WINDOW) & (key_segments[None, :] == query_segments[:, None])
    )
    attended = attend(queries, window_keys, window_values, allowed)
    projected = jnp.dot(
        lax.all_gather(attended, "tp", axis=1, tiled=True),
        out_weight,
        preferred_element_type=jnp.float32,
    )
    return projected.astype(jnp.bfloat16)


def solution(mesh):
    return jax.shard_map(
        shards,
        mesh=mesh,
        in_specs=(
            P("seq", None),
            P(),
            P(None, "tp"),
            P(None, "tp"),
            P(None, "tp"),
            P(None, "tp"),
            P(),
        ),
        out_specs=P("seq", "tp"),
        check_vma=False,
    )
```

profile of v0, /device:TPU:1, one launch (start us, length us, event | category | flops | bytes accessed | tf_op | source)
XLA Modules:
  0.0 180.7 jit_solution(8147630564713881535)
XLA Ops:
  6.5 0.0 copy-start
  6.5 0.0 copy-start.15
  6.5 0.0 all-gather.2.cloned.1.call-start
  6.6 0.0 copy-start.2
  6.6 3.2 %fusion.6 = f32[512]{0:T(512)S(1)} fusion(bf16[512,4096]{1,0:T(8,128)(2,1)} %param.7), kind=kLoop, calls=%fused_computation.13 | loop fusion | flops 6290944 | bytes 4196352 | tf_op jit(solution)/shard_map/reduce_sum | solution.py:60
  9.8 0.0 copy-done
  9.8 0.0 copy-done.15
  9.8 0.5 copy-done.2
  10.3 0.0 copy-start.14
  10.3 1.6 convolution_convert_fusion.1
  11.9 0.0 copy-done.14
  12.0 0.0 copy-start.12
  12.0 1.6 convolution_bitcast_fusion
  13.6 0.0 copy-start.16
  13.6 0.6 fusion.25
  14.2 0.0 copy-start.8
  14.2 0.0 copy-start.10
  14.2 0.7 pad_maximum_fusion
  14.9 4.0 %collective-permute-start.1 = (bf16[512,256]{0,1:T(8,128)(2,1)}, bf16[512,256]{0,1:T(8,128)(2,1)S(1)}, u32[]{:S(2)}, u32[]{:S(2)}) collective-permute-start(bf16[512,256]{0,1:T(8,128)(2,1)} %pad_maximum_fusion), channel_id=1, source_target_pairs={{0,8},{8,16},{16,24},{24,32},{32,40},{40,48},{48,56},{56,64},{64,7... | collective-permute-start | bytes 786440 | tf_op jit(solution)/shard_map/ppermute | solution.py:14
  18.9 5.6 %collective-permute-start = (bf16[512,256]{0,1:T(8,128)(2,1)}, bf16[512,256]{0,1:T(8,128)(2,1)}, u32[]{:S(2)}, u32[]{:S(2)}) collective-permute-start(bf16[512,256]{0,1:T(8,128)(2,1)} %pad_maximum_fusion), channel_id=1, source_target_pairs={{0,64},{8,72},{16,80},{24,88},{32,96},{40,104},{48,112},{56,120},{... | collective-permute-start | bytes 786440 | tf_op jit(solution)/shard_map/ppermute | solution.py:14
  24.5 0.0 copy-done.12
  24.5 0.0 copy-start.3
  24.5 0.1 dynamic_slice.7
  24.6 0.1 pad_dynamic-slice_fusion
  24.7 0.0 collective-permute-done.1
  24.7 0.0 copy-start.4
  24.7 0.1 maximum_maximum_fusion.1
  24.8 5.3 %collective-permute-start.2 = (bf16[1024,256]{0,1:T(8,128)(2,1)S(1)}, bf16[1024,256]{0,1:T(8,128)(2,1)S(1)}, u32[]{:S(2)}, u32[]{:S(2)}) collective-permute-start(bf16[1024,256]{0,1:T(8,128)(2,1)S(1)} %maximum_maximum_fusion.1), channel_id=1, source_target_pairs={{0,16},{8,24},{16,32},{24,40},{32,48},{40,56},{48,64},{56,72},{64,... | collective-permute-start | bytes 1572872 | tf_op jit(solution)/shard_map/ppermute | solution.py:14
  30.1 3.8 %fusion.5 = pred[512,4608]{0,1:T(8,128)(4,1)S(1)} fusion(s32[512]{0:T(512)S(1)} %dynamic_slice.7, s32[4608]{0:T(1024)S(1)} %get-tuple-element.16, s32[512]{0:T(512)S(1)} %iota_add_fusion.1, s32[4608]{0:T(1024)S(1)} %get-tuple-element.15), kind=kLoop, calls=%fused_computation.12 | loop fusion | flops 14155776 | bytes 2400256 | tf_op jit(solution)/shard_map/and | solution.py:92
  33.8 5.9 %collective-permute-done.2 = bf16[1024,256]{0,1:T(8,128)(2,1)S(1)} collective-permute-done((bf16[1024,256]{0,1:T(8,128)(2,1)S(1)}, bf16[1024,256]{0,1:T(8,128)(2,1)S(1)}, u32[]{:S(2)}, u32[]{:S(2)}) %collective-permute-start.2) | collective-permute-done | bytes 524320 | tf_op jit(solution)/shard_map/ppermute | solution.py:14
  39.7 0.0 copy-start.6
  39.7 1.1 maximum_maximum_fusion
  40.9 7.5 %collective-permute-start.3 = (bf16[2048,256]{0,1:T(8,128)(2,1)}, bf16[2048,256]{0,1:T(8,128)(2,1)}, u32[]{:S(2)}, u32[]{:S(2)}) collective-permute-start(bf16[2048,256]{0,1:T(8,128)(2,1)} %maximum_maximum_fusion), channel_id=1, source_target_pairs={{0,32},{8,40},{16,48},{24,56},{32,64},{40,72},{48,80},{56,88},{64,... | collective-permute-start | bytes 3145736 | tf_op jit(solution)/shard_map/ppermute | solution.py:14
  48.4 0.0 copy-done.16
  48.4 0.0 copy-done.3
  48.4 4.8 %fusion.30 = f32[512,512]{0,1:T(8,128)S(1)} fusion(bf16[4096,512]{1,0:T(8,128)(2,1)} %param.9, bf16[512,4096]{1,0:T(8,128)(2,1)S(1)} %copy-done.3, f32[4096]{0:T(1024)S(1)} %copy-done.16, f32[512]{0:T(512)S(1)} %add_rsqrt_fusion), kind=kOutput, calls=%fused_computation.59 | convolution fusion | flops 2155872256 | bytes 9455616 | tf_op jit(solution)/shard_map/dot_general | solution.py:31
  53.2 0.0 copy-done.8
  53.2 0.0 copy-done.10
  53.2 0.0 copy-done.4
  53.2 0.0 copy-done.6
  53.2 1.1 fusion.34
  54.3 1.4 copy.16
  55.6 2.4 %copy.15 = f32[512,4,64]{2,0,1:T(8,128)} copy(f32[512,4,64]{0,2,1:T(8,128)} %get-tuple-element.8) | data formatting | bytes 1048576
  58.0 0.0 copy-start.7
  58.0 1.0 multiply_cosine_fusion
  59.0 1.5 subtract_convert_fusion
  60.5 0.0 collective-permute-done
  60.6 1.0 constant_dynamic-update-slice_fusion.4
  61.5 5.6 %collective-permute-done.3 = bf16[2048,256]{0,1:T(8,128)(2,1)} collective-permute-done((bf16[2048,256]{0,1:T(8,128)(2,1)}, bf16[2048,256]{0,1:T(8,128)(2,1)}, u32[]{:S(2)}, u32[]{:S(2)}) %collective-permute-start.3) | collective-permute-done | bytes 1048608 | tf_op jit(solution)/shard_map/ppermute | solution.py:14
  67.1 1.3 constant_dynamic-update-slice_fusion.3
  68.5 0.0 copy-done.7
  68.5 0.0 copy-done.5
  68.5 0.0 copy-done.9
  68.6 0.0 copy-done.11
  68.6 0.0 copy-start.13
  68.6 15.3 %fusion.1 = (f32[4,512]{1,0:T(4,128)S(1)}, f32[4608,512,4]{1,0,2:T(8,128)}) fusion(pred[512,4608]{0,1:T(8,128)(4,1)S(1)} %fusion.5, bf16[512,4,64]{2,0,1:T(8,128)(2,1)S(1)} %get-tuple-element.6, bf16[512,4,64]{2,0,1:T(8,128)(2,1)S(1)} %get-tuple-element.5, bf16[4608,256]{0,1:T(8,128)(2,1)S(1)} %constant_dynamic-update-slice_fusion), kind=kOutput, calls=%fused_computation.4 | convolution fusion | flops 2445277184 | bytes 42344448 | tf_op jit(solution)/shard_map/tkgd,skd->kgts/dot_general | solution.py:40
  83.9 0.0 copy-done.13
  83.9 16.0 %fusion = f32[4,512]{1,0:T(4,128)S(1)} fusion(f32[4608,512,4]{1,0,2:T(8,128)} %get-tuple-element.14, f32[4,512]{1,0:T(4,128)S(1)} %get-tuple-element.13, pred[512,4608]{0,1:T(8,128)(4,1)S(1)} %fusion.5), kind=kLoop, calls=%fused_computation.3 | loop fusion | flops 37746688 | bytes 40124416 | tf_op jit(solution)/shard_map/reduce_sum | solution.py:46
  99.9 18.3 %fusion.9 = bf16[128,4,512]{2,0,1:T(8,128)(2,1)} fusion(f32[4,512]{1,0:T(4,128)S(1)} %fusion, f32[4,512]{1,0:T(4,128)S(1)} %get-tuple-element.13, f32[4608,512,4]{1,0,2:T(8,128)} %get-tuple-element.14, pred[512,4608]{0,1:T(8,128)(4,1)S(1)} %fusion.5, bf16[4608,256]{0,1:T(8,128)(2,1)} %copy-done.13), kind=kOutput, calls=%fused_computation.17 | convolution fusion | flops 2463367168 | bytes 41828352 | tf_op jit(solution)/shard_map/kgts,skd->tkgd/dot_general | solution.py:48
  118.2 0.0 all-gather.2.cloned.1.call-update
  118.3 0.0 copy-start.1
  118.3 48.9 %all-gather.2.cloned.1.call-done = bf16[512,4096]{0,1:T(8,128)(2,1)} async-done(((bf16[512,512]{0,1:T(8,128)(2,1)}), bf16[512,4096]{0,1:T(8,128)(2,1)}) %all-gather.2.cloned.1.call-update) | async-done | bytes 4194320 | tf_op jit(solution)/shard_map/all_gather | solution.py:96
  167.2 6.6 %convolution_convert_fusion = bf16[512,512]{1,0:T(8,128)(2,1)} fusion(bf16[512,4096]{0,1:T(8,128)(2,1)} %all-gather.2.cloned.1.call-done, bf16[4096,512]{1,0:T(8,128)(2,1)} %param.12), kind=kOutput, calls=%fused_computation.16 | convolution fusion | flops 2147745792 | bytes 8912896 | tf_op jit(solution)/shard_map/dot_general | solution.py:95
  173.8 0.0 copy-done.1
  (10 shorter events, 0.1 us)
Async XLA Ops:
  6.5 3.3 %copy-start = (bf16[4096,128]{1,0:T(8,128)(2,1)S(1)}, bf16[4096,128]{1,0:T(8,128)(2,1)}, u32[]{:S(2)}) copy-start(bf16[4096,128]{1,0:T(8,128)(2,1)} %param.11) | copy-start | bytes 3145732
  6.5 3.3 %copy-start.15 = (f32[4096]{0:T(1024)S(1)}, f32[4096]{0:T(1024)}, u32[]{:S(2)}) copy-start(f32[4096]{0:T(1024)} %param.8) | copy-start | bytes 49156
  6.5 160.7 %all-gather.2.cloned.1.call-start = ((), (), s32[]{:S(2)}) async-start(), calls=%async_computation | async-start | bytes 4718592 | tf_op jit(solution)/shard_map/all_gather | solution.py:96
  6.6 3.8 %copy-start.2 = (bf16[512,4096]{1,0:T(8,128)(2,1)S(1)}, bf16[512,4096]{1,0:T(8,128)(2,1)}, u32[]{:S(2)}) copy-start(bf16[512,4096]{1,0:T(8,128)(2,1)} %param.7) | copy-start | bytes 12582916
  10.3 1.6 copy-start.14
  12.0 12.6 %copy-start.12 = (s32[16384]{0:T(1024)S(1)}, s32[16384]{0:T(1024)}, u32[]{:S(2)}) copy-start(s32[16384]{0:T(1024)} %param.13) | copy-start | bytes 196612
  13.6 34.8 %copy-start.16 = (f32[4096]{0:T(1024)S(1)}, f32[4096]{0:T(1024)}, u32[]{:S(2)}) copy-start(f32[4096]{0:T(1024)} %param.8) | copy-start | bytes 49156
  14.2 39.0 %copy-start.8 = (bf16[512,64]{0,1:T(8,128)(2,1)}, bf16[512,64]{0,1:T(8,128)(2,1)S(1)}, u32[]{:S(2)}) copy-start(bf16[512,64]{0,1:T(8,128)(2,1)S(1)} %get-tuple-element.9) | copy-start | bytes 196612
  14.2 39.0 %copy-start.10 = (bf16[512,64]{0,1:T(8,128)(2,1)}, bf16[512,64]{0,1:T(8,128)(2,1)S(1)}, u32[]{:S(2)}) copy-start(bf16[512,64]{0,1:T(8,128)(2,1)S(1)} %get-tuple-element.10) | copy-start | bytes 196612
  14.9 9.8 %collective-permute-start.1 = (bf16[512,256]{0,1:T(8,128)(2,1)}, bf16[512,256]{0,1:T(8,128)(2,1)S(1)}, u32[]{:S(2)}, u32[]{:S(2)}) collective-permute-start(bf16[512,256]{0,1:T(8,128)(2,1)} %pad_maximum_fusion), channel_id=1, source_target_pairs={{0,8},{8,16},{16,24},{24,32},{32,40},{40,48},{48,56},{56,64},{64,7... | collective-permute-start | bytes 786440 | tf_op jit(solution)/shard_map/ppermute | solution.py:14
  18.9 41.6 %collective-permute-start = (bf16[512,256]{0,1:T(8,128)(2,1)}, bf16[512,256]{0,1:T(8,128)(2,1)}, u32[]{:S(2)}, u32[]{:S(2)}) collective-permute-start(bf16[512,256]{0,1:T(8,128)(2,1)} %pad_maximum_fusion), channel_id=1, source_target_pairs={{0,64},{8,72},{16,80},{24,88},{32,96},{40,104},{48,112},{56,120},{... | collective-permute-start | bytes 786440 | tf_op jit(solution)/shard_map/ppermute | solution.py:14
  24.5 23.9 %copy-start.3 = (bf16[512,4096]{1,0:T(8,128)(2,1)S(1)}, bf16[512,4096]{1,0:T(8,128)(2,1)}, u32[]{:S(2)}) copy-start(bf16[512,4096]{1,0:T(8,128)(2,1)} %param.7) | copy-start | bytes 12582916
  24.7 28.5 %copy-start.4 = (bf16[512,256]{0,1:T(8,128)(2,1)}, bf16[512,256]{0,1:T(8,128)(2,1)S(1)}, u32[]{:S(2)}) copy-start(bf16[512,256]{0,1:T(8,128)(2,1)S(1)} %collective-permute-done.1) | copy-start | bytes 786436
  24.8 15.0 %collective-permute-start.2 = (bf16[1024,256]{0,1:T(8,128)(2,1)S(1)}, bf16[1024,256]{0,1:T(8,128)(2,1)S(1)}, u32[]{:S(2)}, u32[]{:S(2)}) collective-permute-start(bf16[1024,256]{0,1:T(8,128)(2,1)S(1)} %maximum_maximum_fusion.1), channel_id=1, source_target_pairs={{0,16},{8,24},{16,32},{24,40},{32,48},{40,56},{48,64},{56,72},{64,... | collective-permute-start | bytes 1572872 | tf_op jit(solution)/shard_map/ppermute | solution.py:14
  39.7 13.5 %copy-start.6 = (bf16[1024,256]{0,1:T(8,128)(2,1)}, bf16[1024,256]{0,1:T(8,128)(2,1)S(1)}, u32[]{:S(2)}) copy-start(bf16[1024,256]{0,1:T(8,128)(2,1)S(1)} %collective-permute-done.2) | copy-start | bytes 1572868
  40.9 26.3 %collective-permute-start.3 = (bf16[2048,256]{0,1:T(8,128)(2,1)}, bf16[2048,256]{0,1:T(8,128)(2,1)}, u32[]{:S(2)}, u32[]{:S(2)}) collective-permute-start(bf16[2048,256]{0,1:T(8,128)(2,1)} %maximum_maximum_fusion), channel_id=1, source_target_pairs={{0,32},{8,40},{16,48},{24,56},{32,64},{40,72},{48,80},{56,88},{64,... | collective-permute-start | bytes 3145736 | tf_op jit(solution)/shard_map/ppermute | solution.py:14
  58.0 10.4 %copy-start.7 = (bf16[1024,256]{0,1:T(8,128)(2,1)S(1)}, bf16[1024,256]{0,1:T(8,128)(2,1)}, u32[]{:S(2)}) copy-start(bf16[1024,256]{0,1:T(8,128)(2,1)} %copy-done.6) | copy-start | bytes 1572868
  58.0 10.5 %copy-start.5 = (bf16[512,256]{0,1:T(8,128)(2,1)S(1)}, bf16[512,256]{0,1:T(8,128)(2,1)}, u32[]{:S(2)}) copy-start(bf16[512,256]{0,1:T(8,128)(2,1)} %copy-done.4) | copy-start | bytes 786436
  58.0 10.5 %copy-start.9 = (bf16[512,64]{0,1:T(8,128)(2,1)S(1)}, bf16[512,64]{0,1:T(8,128)(2,1)}, u32[]{:S(2)}) copy-start(bf16[512,64]{0,1:T(8,128)(2,1)} %copy-done.8) | copy-start | bytes 196612
  58.0 10.5 %copy-start.11 = (bf16[512,64]{0,1:T(8,128)(2,1)S(1)}, bf16[512,64]{0,1:T(8,128)(2,1)}, u32[]{:S(2)}) copy-start(bf16[512,64]{0,1:T(8,128)(2,1)} %copy-done.10) | copy-start | bytes 196612
  68.6 15.3 %copy-start.13 = (bf16[4608,256]{0,1:T(8,128)(2,1)}, bf16[4608,256]{0,1:T(8,128)(2,1)S(1)}, u32[]{:S(2)}) copy-start(bf16[4608,256]{0,1:T(8,128)(2,1)S(1)} %constant_dynamic-update-slice_fusion) | copy-start | bytes 7077892
  118.3 55.5 %copy-start.1 = (bf16[4096,128]{1,0:T(8,128)(2,1)S(1)}, bf16[4096,128]{1,0:T(8,128)(2,1)}, u32[]{:S(2)}) copy-start(bf16[4096,128]{1,0:T(8,128)(2,1)} %param.11) | copy-start | bytes 3145732
Sparse Core Ops, SparseCore 0:
  118.4 48.7 all-gather.1
where the time goes:
time: 181 us
  waiting for transfers between devices  60.5 us (33%)
  matrix products  48.2 us (27%)
  other arithmetic  28.1 us (16%)
  starting transfers between devices  22.4 us (12%)
  between operations  13.7 us (8%)
  local copies, waits for them, and re-layouts  7.74 us (4%)
    all_gather x1, waiting for transfers between devices, shards(): lax.all_gather(attended, 'tp', axis=1, tiled=True)  48.9 us
    ppermute x4, starting transfers between devices, shifted(): lax.ppermute(value, axis, [(source, source + steps) for source in range(l...  22.4 us
    dot_general x1, matrix products, attend(): jnp.einsum('kgts,skd->tkgd', probabilities, values, preferred_element_typ...  18.3 us
    reduce_sum x1, other arithmetic, attend(): totals = jnp.sum(weights, axis=-1, keepdims=True)  16 us
    dot_general x1, matrix products, attend(): jnp.einsum('tkgd,skd->kgts', grouped, keys, preferred_element_type=jnp.fl...  15.3 us
    ppermute x4, waiting for transfers between devices, shifted(): lax.ppermute(value, axis, [(source, source + steps) for source in range(l...  11.6 us
    unnamed x40, local copies, waits for them, and re-layouts  6.61 us
    dot_general x1, matrix products, shards(): jnp.dot(lax.all_gather(attended, 'tp', axis=1, tiled=True), out_weight, p...  6.61 us
  transfers between devices with their start and end apart: 5, of which 3 were waited for; matrix products, arithmetic and copies ran while one was open for 10% of the time, Pallas kernels for 0%

commit v1 on v0

--- a/solution.py
+++ b/solution.py
@@ -6,6 +6,19 @@
 
 HEAD_DIM = 128
 WINDOW = 4096
+
+
+def ring_gather(x, axis, dim):
+    ways = lax.axis_size(axis)
+    up = [(d, (d + 1) % ways) for d in range(ways)]
+    down = [(d, (d - 1) % ways) for d in range(ways)]
+    earlier, later = ([x], [x])
+    for _ in range(ways // 2):
+        earlier.append(lax.ppermute(earlier[-1], axis, up))
+    for _ in range((ways - 1) // 2):
+        later.append(lax.ppermute(later[-1], axis, down))
+    line = jnp.concatenate([*earlier[::-1], *later[1:]], axis=dim)
+    return jnp.roll(line, (lax.axis_index(axis) - ways // 2) * x.shape[dim], axis=dim)
 
 
 def shifted(value, axis, steps):
@@ -93,9 +106,7 @@
     )
     attended = attend(queries, window_keys, window_values, allowed)
     projected = jnp.dot(
-        lax.all_gather(attended, "tp", axis=1, tiled=True),
-        out_weight,
-        preferred_element_type=jnp.float32,
+        ring_gather(attended, "tp", 1), out_weight, preferred_element_type=jnp.float32
     )
     return projected.astype(jnp.bfloat16)
 

time: 181 us -> 172 us (0.950)
  the two profiles are of different devices: /device:TPU:1 before, /device:TPU:136 now
where the time goes in v1:
time: 172 us
  waiting for transfers between devices  61.9 us (36%)
  matrix products  47.4 us (28%)
  other arithmetic  28.2 us (16%)
  starting transfers between devices  21.9 us (13%)
  local copies, waits for them, and re-layouts  11.9 us (7%)
    ppermute x4, waiting for transfers between devices, shifted(): lax.ppermute(value, axis, [(source, source + steps) for source in range(l...  31.4 us
    ppermute x4, waiting for transfers between devices, ring_gather(): earlier.append(lax.ppermute(earlier[-1], axis, up))  30.5 us
    dot_general x1, matrix products, attend(): jnp.einsum('kgts,skd->tkgd', probabilities, values, preferred_element_typ...  17.6 us
    reduce_sum x1, other arithmetic, attend(): totals = jnp.sum(weights, axis=-1, keepdims=True)  16 us
    dot_general x1, matrix products, attend(): jnp.einsum('tkgd,skd->kgts', grouped, keys, preferred_element_type=jnp.fl...  15.3 us
    ppermute x4, starting transfers between devices, shifted(): lax.ppermute(value, axis, [(source, source + steps) for source in range(l...  13 us
    unnamed x51, local copies, waits for them, and re-layouts  10.7 us
    ppermute x3, starting transfers between devices, ring_gather(): later.append(lax.ppermute(later[-1], axis, down))  8.86 us
  transfers between devices with their start and end apart: 11, of which 7 were waited for; matrix products, arithmetic and copies ran while one was open for 12% of the time, Pallas kernels for 0%

profile of v1, /device:TPU:136, one launch (start us, length us, event | category | flops | bytes accessed | tf_op | source)
XLA Modules:
  0.0 171.7 jit_solution(16664720759393424545)
XLA Ops:
  0.0 0.0 copy-start
  0.0 0.0 copy-start.2
  0.1 3.2 %fusion.6 = f32[512]{0:T(512)S(1)} fusion(bf16[512,4096]{1,0:T(8,128)(2,1)} %param.7), kind=kLoop, calls=%fused_computation.13 | loop fusion | flops 6290944 | bytes 4196352 | tf_op jit(solution)/shard_map/reduce_sum | solution.py:73
  3.3 0.0 copy-done
  3.3 3.8 %convolution_convert_fusion = bf16[512,128]{0,1:T(8,128)(2,1)S(1)} fusion(bf16[4096,128]{1,0:T(8,128)(2,1)S(1)} %copy-done, bf16[512,4096]{1,0:T(8,128)(2,1)} %param.7, f32[4096]{0:T(1024)} %param.8, f32[512]{0:T(512)S(1)} %add_rsqrt_fusion), kind=kOutput, calls=%fused_computation.24 | convolution fusion | flops 545325056 | bytes 5392384 | tf_op jit(solution)/shard_map/dot_general | solution.py:80
  7.1 0.0 copy-done.13
  7.1 0.0 copy-done.12
  7.1 0.0 copy-done.2
  7.1 0.0 copy-start.9
  7.2 0.0 copy-start.14
  7.2 1.6 convolution_bitcast_fusion
  8.8 0.6 fusion.30
  9.3 0.0 copy-start.5
  9.4 0.0 copy-start.7
  9.4 0.8 pad_maximum_fusion
  10.1 3.5 %collective-permute-start.1 = (bf16[512,256]{0,1:T(8,128)(2,1)}, bf16[512,256]{0,1:T(8,128)(2,1)S(1)}, u32[]{:S(2)}, u32[]{:S(2)}) collective-permute-start(bf16[512,256]{0,1:T(8,128)(2,1)} %pad_maximum_fusion), channel_id=1, source_target_pairs={{0,8},{8,16},{16,24},{24,32},{32,40},{40,48},{48,56},{56,64},{64,7... | collective-permute-start | bytes 786440 | tf_op jit(solution)/shard_map/ppermute | solution.py:27
  13.6 3.4 %collective-permute-start = (bf16[512,256]{0,1:T(8,128)(2,1)}, bf16[512,256]{0,1:T(8,128)(2,1)}, u32[]{:S(2)}, u32[]{:S(2)}) collective-permute-start(bf16[512,256]{0,1:T(8,128)(2,1)} %pad_maximum_fusion), channel_id=1, source_target_pairs={{0,64},{8,72},{16,80},{24,88},{32,96},{40,104},{48,112},{56,120},{... | collective-permute-start | bytes 786440 | tf_op jit(solution)/shard_map/ppermute | solution.py:27
  17.0 0.0 copy-done.9
  17.0 0.1 dynamic_slice.11
  17.1 0.1 pad_dynamic-slice_fusion
  17.2 3.1 %collective-permute-done.1 = bf16[512,256]{0,1:T(8,128)(2,1)S(1)} collective-permute-done((bf16[512,256]{0,1:T(8,128)(2,1)}, bf16[512,256]{0,1:T(8,128)(2,1)S(1)}, u32[]{:S(2)}, u32[]{:S(2)}) %collective-permute-start.1) | collective-permute-done | bytes 262176 | tf_op jit(solution)/shard_map/ppermute | solution.py:27
  20.3 0.1 maximum_maximum_fusion.1
  20.3 4.2 %collective-permute-start.2 = (bf16[1024,256]{0,1:T(8,128)(2,1)S(1)}, bf16[1024,256]{0,1:T(8,128)(2,1)S(1)}, u32[]{:S(2)}, u32[]{:S(2)}) collective-permute-start(bf16[1024,256]{0,1:T(8,128)(2,1)S(1)} %maximum_maximum_fusion.1), channel_id=1, source_target_pairs={{0,16},{8,24},{16,32},{24,40},{32,48},{40,56},{48,64},{56,72},{64,... | collective-permute-start | bytes 1572872 | tf_op jit(solution)/shard_map/ppermute | solution.py:27
  24.5 3.8 %fusion.5 = pred[512,4608]{0,1:T(8,128)(4,1)S(1)} fusion(s32[512]{0:T(512)S(1)} %dynamic_slice.11, s32[4608]{0:T(1024)S(1)} %get-tuple-element.16, s32[512]{0:T(512)S(1)} %iota_add_fusion.1, s32[4608]{0:T(1024)S(1)} %get-tuple-element.15), kind=kLoop, calls=%fused_computation.12 | loop fusion | flops 14155776 | bytes 2400256 | tf_op jit(solution)/shard_map/and | solution.py:105
  28.3 17.1 %collective-permute-done.2 = bf16[1024,256]{0,1:T(8,128)(2,1)S(1)} collective-permute-done((bf16[1024,256]{0,1:T(8,128)(2,1)S(1)}, bf16[1024,256]{0,1:T(8,128)(2,1)S(1)}, u32[]{:S(2)}, u32[]{:S(2)}) %collective-permute-start.2) | collective-permute-done | bytes 524320 | tf_op jit(solution)/shard_map/ppermute | solution.py:27
  45.4 1.1 maximum_maximum_fusion
  46.5 1.9 %collective-permute-start.3 = (bf16[2048,256]{0,1:T(8,128)(2,1)}, bf16[2048,256]{0,1:T(8,128)(2,1)}, u32[]{:S(2)}, u32[]{:S(2)}) collective-permute-start(bf16[2048,256]{0,1:T(8,128)(2,1)} %maximum_maximum_fusion), channel_id=1, source_target_pairs={{0,32},{8,40},{16,48},{24,56},{32,64},{40,72},{48,80},{56,88},{64,... | collective-permute-start | bytes 3145736 | tf_op jit(solution)/shard_map/ppermute | solution.py:27
  48.5 0.0 copy-done.14
  48.5 5.9 %fusion.36 = f32[512,512]{0,1:T(8,128)S(1)} fusion(bf16[4096,512]{1,0:T(8,128)(2,1)} %param.9, bf16[512,4096]{1,0:T(8,128)(2,1)} %param.7, f32[4096]{0:T(1024)S(1)} %copy-done.14, f32[512]{0:T(512)S(1)} %add_rsqrt_fusion), kind=kOutput, calls=%fused_computation.78 | convolution fusion | flops 2155872256 | bytes 9455616 | tf_op jit(solution)/shard_map/dot_general | solution.py:44
  54.4 1.1 fusion.40
  55.5 1.4 copy.16
  56.9 2.4 %copy.15 = f32[512,4,64]{2,0,1:T(8,128)} copy(f32[512,4,64]{0,2,1:T(8,128)} %get-tuple-element.8) | data formatting | bytes 1048576
  59.2 1.0 multiply_cosine_fusion
  60.2 1.5 subtract_convert_fusion
  61.8 0.0 collective-permute-done
  61.8 1.0 constant_dynamic-update-slice_fusion.4
  62.8 11.2 %collective-permute-done.3 = bf16[2048,256]{0,1:T(8,128)(2,1)} collective-permute-done((bf16[2048,256]{0,1:T(8,128)(2,1)}, bf16[2048,256]{0,1:T(8,128)(2,1)}, u32[]{:S(2)}, u32[]{:S(2)}) %collective-permute-start.3) | collective-permute-done | bytes 1048608 | tf_op jit(solution)/shard_map/ppermute | solution.py:27
  74.0 1.3 constant_dynamic-update-slice_fusion.3
  75.3 1.1 constant_dynamic-update-slice_fusion.2
  76.4 1.0 constant_dynamic-update-slice_fusion.1
  77.4 0.0 copy-done.6
  77.4 0.0 copy-done.8
  77.4 15.3 %fusion.1 = (f32[4,512]{1,0:T(4,128)S(1)}, f32[4608,512,4]{1,0,2:T(8,128)}) fusion(pred[512,4608]{0,1:T(8,128)(4,1)S(1)} %fusion.5, bf16[512,4,64]{2,0,1:T(8,128)(2,1)S(1)} %get-tuple-element.6, bf16[512,4,64]{2,0,1:T(8,128)(2,1)S(1)} %get-tuple-element.5, bf16[4608,256]{0,1:T(8,128)(2,1)S(1)} %constant_dynamic-update-slice_fusion), kind=kOutput, calls=%fused_computation.4 | convolution fusion | flops 2445277184 | bytes 42344448 | tf_op jit(solution)/shard_map/tkgd,skd->kgts/dot_general | solution.py:53
  92.7 0.0 copy-done.10
  92.7 16.0 %fusion = f32[4,512]{1,0:T(4,128)S(1)} fusion(f32[4608,512,4]{1,0,2:T(8,128)} %get-tuple-element.14, f32[4,512]{1,0:T(4,128)S(1)} %get-tuple-element.13, pred[512,4608]{0,1:T(8,128)(4,1)S(1)} %fusion.5), kind=kLoop, calls=%fused_computation.3 | loop fusion | flops 37746688 | bytes 40124416 | tf_op jit(solution)/shard_map/reduce_sum | solution.py:59
  108.7 17.6 %fusion.14 = bf16[128,4,512]{2,0,1:T(8,128)(2,1)S(1)} fusion(f32[4,512]{1,0:T(4,128)S(1)} %fusion, f32[4,512]{1,0:T(4,128)S(1)} %get-tuple-element.13, f32[4608,512,4]{1,0,2:T(8,128)} %get-tuple-element.14, pred[512,4608]{0,1:T(8,128)(4,1)S(1)} %fusion.5, bf16[4608,256]{0,1:T(8,128)(2,1)} %copy-done.10), kind=kOutput, calls=%fused_computation.19 | convolution fusion | flops 2463367168 | bytes 41828352 | tf_op jit(solution)/shard_map/kgts,skd->tkgd/dot_general | solution.py:61
  126.4 0.0 collective-permute-start.4
  126.4 9.8 %collective-permute-done.4 = bf16[512,512]{0,1:T(8,128)(2,1)S(1)} collective-permute-done((bf16[512,512]{0,1:T(8,128)(2,1)S(1)}, bf16[512,512]{0,1:T(8,128)(2,1)S(1)}, u32[]{:S(2)}, u32[]{:S(2)}) %collective-permute-start.4) | collective-permute-done | bytes 524320 | tf_op jit(solution)/shard_map/ppermute | solution.py:17
  136.2 0.0 collective-permute-start.5
  136.2 3.0 %collective-permute-start.8 = (bf16[512,512]{0,1:T(8,128)(2,1)S(1)}, bf16[512,512]{0,1:T(8,128)(2,1)S(1)}, u32[]{:S(2)}, u32[]{:S(2)}) collective-permute-start(bf16[512,512]{0,1:T(8,128)(2,1)S(1)} %bitcast.45), channel_id=1, source_target_pairs={{0,7},{1,0},{2,1},{3,2},{4,3},{5,4},{6,5},{7,6},{8,15},{9,8},{10,9... | collective-permute-start | bytes 1572872 | tf_op jit(solution)/shard_map/ppermute | solution.py:19
  139.2 6.9 %collective-permute-done.5 = bf16[512,512]{0,1:T(8,128)(2,1)S(1)} collective-permute-done((bf16[512,512]{0,1:T(8,128)(2,1)S(1)}, bf16[512,512]{0,1:T(8,128)(2,1)S(1)}, u32[]{:S(2)}, u32[]{:S(2)}) %collective-permute-start.5) | collective-permute-done | bytes 524320 | tf_op jit(solution)/shard_map/ppermute | solution.py:17
  146.0 0.0 collective-permute-start.6
  146.0 0.0 collective-permute-done.8
  146.0 3.0 %collective-permute-start.9 = (bf16[512,512]{0,1:T(8,128)(2,1)S(1)}, bf16[512,512]{0,1:T(8,128)(2,1)S(1)}, u32[]{:S(2)}, u32[]{:S(2)}) collective-permute-start(bf16[512,512]{0,1:T(8,128)(2,1)S(1)} %collective-permute-done.8), channel_id=1, source_target_pairs={{0,7},{1,0},{2,1},{3,2},{4,3},{5,4},{6,5},{7,6},{8,15},{9,8},{10,9... | collective-permute-start | bytes 1572872 | tf_op jit(solution)/shard_map/ppermute | solution.py:19
  149.0 6.9 %collective-permute-done.6 = bf16[512,512]{0,1:T(8,128)(2,1)S(1)} collective-permute-done((bf16[512,512]{0,1:T(8,128)(2,1)S(1)}, bf16[512,512]{0,1:T(8,128)(2,1)S(1)}, u32[]{:S(2)}, u32[]{:S(2)}) %collective-permute-start.6) | collective-permute-done | bytes 524320 | tf_op jit(solution)/shard_map/ppermute | solution.py:17
  155.8 0.0 collective-permute-start.7
  155.8 0.0 collective-permute-done.9
  155.8 3.0 %collective-permute-start.10 = (bf16[512,512]{0,1:T(8,128)(2,1)S(1)}, bf16[512,512]{0,1:T(8,128)(2,1)S(1)}, u32[]{:S(2)}, u32[]{:S(2)}) collective-permute-start(bf16[512,512]{0,1:T(8,128)(2,1)S(1)} %collective-permute-done.9), channel_id=1, source_target_pairs={{0,7},{1,0},{2,1},{3,2},{4,3},{5,4},{6,5},{7,6},{8,15},{9,8},{10,9... | collective-permute-start | bytes 1572872 | tf_op jit(solution)/shard_map/ppermute | solution.py:19
  158.8 7.0 %collective-permute-done.7 = bf16[512,512]{0,1:T(8,128)(2,1)} collective-permute-done((bf16[512,512]{0,1:T(8,128)(2,1)S(1)}, bf16[512,512]{0,1:T(8,128)(2,1)}, u32[]{:S(2)}, u32[]{:S(2)}) %collective-permute-start.7) | collective-permute-done | bytes 524320 | tf_op jit(solution)/shard_map/ppermute | solution.py:17
  165.8 1.1 constant_dynamic-update-slice_fusion.20
  167.1 0.0 collective-permute-done.10
  167.2 1.1 constant_dynamic-update-slice_fusion.12
  168.5 0.0 copy-start.1
  168.6 3.2 %fusion.11 = bf16[512,512]{1,0:T(8,128)(2,1)} fusion(bf16[4096,512]{1,0:T(8,128)(2,1)S(1)} %copy-done.11, bf16[512,8192]{0,1:T(8,128)(2,1)S(1)} %constant_dynamic-update-slice_fusion.5, s32[]{:T(128)S(6)} %select_n.27), kind=kOutput, calls=%fused_computation.18 | convolution fusion | flops 2147745792 | bytes 8912900 | tf_op jit(solution)/shard_map/dot_general | solution.py:108
  (33 shorter events, 0.6 us)
Async XLA Ops:
  0.0 3.3 %copy-start = (bf16[4096,128]{1,0:T(8,128)(2,1)S(1)}, bf16[4096,128]{1,0:T(8,128)(2,1)}, u32[]{:S(2)}) copy-start(bf16[4096,128]{1,0:T(8,128)(2,1)} %param.11) | copy-start | bytes 3145732
  0.0 7.1 %copy-start.13 = (f32[4096]{0:T(1024)S(1)}, f32[4096]{0:T(1024)}, u32[]{:S(2)}) copy-start(f32[4096]{0:T(1024)} %param.8) | copy-start | bytes 49156
  0.0 7.1 %copy-start.12 = (bf16[4096,128]{1,0:T(8,128)(2,1)S(1)}, bf16[4096,128]{1,0:T(8,128)(2,1)}, u32[]{:S(2)}) copy-start(bf16[4096,128]{1,0:T(8,128)(2,1)} %param.10) | copy-start | bytes 3145732
  0.0 7.1 %copy-start.2 = (bf16[512,4096]{1,0:T(8,128)(2,1)S(1)}, bf16[512,4096]{1,0:T(8,128)(2,1)}, u32[]{:S(2)}) copy-start(bf16[512,4096]{1,0:T(8,128)(2,1)} %param.7) | copy-start | bytes 12582916
  7.1 9.9 %copy-start.9 = (s32[16384]{0:T(1024)S(1)}, s32[16384]{0:T(1024)}, u32[]{:S(2)}) copy-start(s32[16384]{0:T(1024)} %param.13) | copy-start | bytes 196612
  7.2 41.3 %copy-start.14 = (f32[4096]{0:T(1024)S(1)}, f32[4096]{0:T(1024)}, u32[]{:S(2)}) copy-start(f32[4096]{0:T(1024)} %param.8) | copy-start | bytes 49156
  9.3 45.1 %copy-start.5 = (bf16[512,64]{0,1:T(8,128)(2,1)}, bf16[512,64]{0,1:T(8,128)(2,1)S(1)}, u32[]{:S(2)}) copy-start(bf16[512,64]{0,1:T(8,128)(2,1)S(1)} %get-tuple-element.9) | copy-start | bytes 196612
  9.4 45.1 %copy-start.7 = (bf16[512,64]{0,1:T(8,128)(2,1)}, bf16[512,64]{0,1:T(8,128)(2,1)S(1)}, u32[]{:S(2)}) copy-start(bf16[512,64]{0,1:T(8,128)(2,1)S(1)} %get-tuple-element.10) | copy-start | bytes 196612
  10.1 10.1 %collective-permute-start.1 = (bf16[512,256]{0,1:T(8,128)(2,1)}, bf16[512,256]{0,1:T(8,128)(2,1)S(1)}, u32[]{:S(2)}, u32[]{:S(2)}) collective-permute-start(bf16[512,256]{0,1:T(8,128)(2,1)} %pad_maximum_fusion), channel_id=1, source_target_pairs={{0,8},{8,16},{16,24},{24,32},{32,40},{40,48},{48,56},{56,64},{64,7... | collective-permute-start | bytes 786440 | tf_op jit(solution)/shard_map/ppermute | solution.py:27
  13.6 48.2 %collective-permute-start = (bf16[512,256]{0,1:T(8,128)(2,1)}, bf16[512,256]{0,1:T(8,128)(2,1)}, u32[]{:S(2)}, u32[]{:S(2)}) collective-permute-start(bf16[512,256]{0,1:T(8,128)(2,1)} %pad_maximum_fusion), channel_id=1, source_target_pairs={{0,64},{8,72},{16,80},{24,88},{32,96},{40,104},{48,112},{56,120},{... | collective-permute-start | bytes 786440 | tf_op jit(solution)/shard_map/ppermute | solution.py:27
  20.3 34.2 %copy-start.3 = (bf16[512,256]{0,1:T(8,128)(2,1)}, bf16[512,256]{0,1:T(8,128)(2,1)S(1)}, u32[]{:S(2)}) copy-start(bf16[512,256]{0,1:T(8,128)(2,1)S(1)} %collective-permute-done.1) | copy-start | bytes 786436
  20.3 25.1 %collective-permute-start.2 = (bf16[1024,256]{0,1:T(8,128)(2,1)S(1)}, bf16[1024,256]{0,1:T(8,128)(2,1)S(1)}, u32[]{:S(2)}, u32[]{:S(2)}) collective-permute-start(bf16[1024,256]{0,1:T(8,128)(2,1)S(1)} %maximum_maximum_fusion.1), channel_id=1, source_target_pairs={{0,16},{8,24},{16,32},{24,40},{32,48},{40,56},{48,64},{56,72},{64,... | collective-permute-start | bytes 1572872 | tf_op jit(solution)/shard_map/ppermute | solution.py:27
  45.4 9.0 %copy-start.4 = (bf16[1024,256]{0,1:T(8,128)(2,1)}, bf16[1024,256]{0,1:T(8,128)(2,1)S(1)}, u32[]{:S(2)}) copy-start(bf16[1024,256]{0,1:T(8,128)(2,1)S(1)} %collective-permute-done.2) | copy-start | bytes 1572868
  46.5 27.5 %collective-permute-start.3 = (bf16[2048,256]{0,1:T(8,128)(2,1)}, bf16[2048,256]{0,1:T(8,128)(2,1)}, u32[]{:S(2)}, u32[]{:S(2)}) collective-permute-start(bf16[2048,256]{0,1:T(8,128)(2,1)} %maximum_maximum_fusion), channel_id=1, source_target_pairs={{0,32},{8,40},{16,48},{24,56},{32,64},{40,72},{48,80},{56,88},{64,... | collective-permute-start | bytes 3145736 | tf_op jit(solution)/shard_map/ppermute | solution.py:27
  59.2 18.1 %copy-start.6 = (bf16[512,64]{0,1:T(8,128)(2,1)S(1)}, bf16[512,64]{0,1:T(8,128)(2,1)}, u32[]{:S(2)}) copy-start(bf16[512,64]{0,1:T(8,128)(2,1)} %copy-done.5) | copy-start | bytes 196612
  59.2 18.1 %copy-start.8 = (bf16[512,64]{0,1:T(8,128)(2,1)S(1)}, bf16[512,64]{0,1:T(8,128)(2,1)}, u32[]{:S(2)}) copy-start(bf16[512,64]{0,1:T(8,128)(2,1)} %copy-done.7) | copy-start | bytes 196612
  77.4 15.3 %copy-start.10 = (bf16[4608,256]{0,1:T(8,128)(2,1)}, bf16[4608,256]{0,1:T(8,128)(2,1)S(1)}, u32[]{:S(2)}) copy-start(bf16[4608,256]{0,1:T(8,128)(2,1)S(1)} %constant_dynamic-update-slice_fusion) | copy-start | bytes 7077892
  126.4 9.8 %collective-permute-start.4 = (bf16[512,512]{0,1:T(8,128)(2,1)S(1)}, bf16[512,512]{0,1:T(8,128)(2,1)S(1)}, u32[]{:S(2)}, u32[]{:S(2)}) collective-permute-start(bf16[512,512]{0,1:T(8,128)(2,1)S(1)} %bitcast.44), channel_id=1, source_target_pairs={{0,1},{1,2},{2,3},{3,4},{4,5},{5,6},{6,7},{7,0},{8,9},{9,10},{10,1... | collective-permute-start | bytes 1572872 | tf_op jit(solution)/shard_map/ppermute | solution.py:17
  136.2 9.8 %collective-permute-start.5 = (bf16[512,512]{0,1:T(8,128)(2,1)S(1)}, bf16[512,512]{0,1:T(8,128)(2,1)S(1)}, u32[]{:S(2)}, u32[]{:S(2)}) collective-permute-start(bf16[512,512]{0,1:T(8,128)(2,1)S(1)} %collective-permute-done.4), channel_id=1, source_target_pairs={{0,1},{1,2},{2,3},{3,4},{4,5},{5,6},{6,7},{7,0},{8,9},{9,10},{10,1... | collective-permute-start | bytes 1572872 | tf_op jit(solution)/shard_map/ppermute | solution.py:17
  136.2 9.8 %collective-permute-start.8 = (bf16[512,512]{0,1:T(8,128)(2,1)S(1)}, bf16[512,512]{0,1:T(8,128)(2,1)S(1)}, u32[]{:S(2)}, u32[]{:S(2)}) collective-permute-start(bf16[512,512]{0,1:T(8,128)(2,1)S(1)} %bitcast.45), channel_id=1, source_target_pairs={{0,7},{1,0},{2,1},{3,2},{4,3},{5,4},{6,5},{7,6},{8,15},{9,8},{10,9... | collective-permute-start | bytes 1572872 | tf_op jit(solution)/shard_map/ppermute | solution.py:19
  146.0 9.8 %collective-permute-start.6 = (bf16[512,512]{0,1:T(8,128)(2,1)S(1)}, bf16[512,512]{0,1:T(8,128)(2,1)S(1)}, u32[]{:S(2)}, u32[]{:S(2)}) collective-permute-start(bf16[512,512]{0,1:T(8,128)(2,1)S(1)} %collective-permute-done.5), channel_id=1, source_target_pairs={{0,1},{1,2},{2,3},{3,4},{4,5},{5,6},{6,7},{7,0},{8,9},{9,10},{10,1... | collective-permute-start | bytes 1572872 | tf_op jit(solution)/shard_map/ppermute | solution.py:17
  146.0 9.8 %collective-permute-start.9 = (bf16[512,512]{0,1:T(8,128)(2,1)S(1)}, bf16[512,512]{0,1:T(8,128)(2,1)S(1)}, u32[]{:S(2)}, u32[]{:S(2)}) collective-permute-start(bf16[512,512]{0,1:T(8,128)(2,1)S(1)} %collective-permute-done.8), channel_id=1, source_target_pairs={{0,7},{1,0},{2,1},{3,2},{4,3},{5,4},{6,5},{7,6},{8,15},{9,8},{10,9... | collective-permute-start | bytes 1572872 | tf_op jit(solution)/shard_map/ppermute | solution.py:19
  155.8 9.9 %collective-permute-start.7 = (bf16[512,512]{0,1:T(8,128)(2,1)S(1)}, bf16[512,512]{0,1:T(8,128)(2,1)}, u32[]{:S(2)}, u32[]{:S(2)}) collective-permute-start(bf16[512,512]{0,1:T(8,128)(2,1)S(1)} %collective-permute-done.6), channel_id=1, source_target_pairs={{0,1},{1,2},{2,3},{3,4},{4,5},{5,6},{6,7},{7,0},{8,9},{9,10},{10,1... | collective-permute-start | bytes 1572872 | tf_op jit(solution)/shard_map/ppermute | solution.py:17
  155.8 12.7 %copy-start.11 = (bf16[4096,512]{1,0:T(8,128)(2,1)S(1)}, bf16[4096,512]{1,0:T(8,128)(2,1)}, u32[]{:S(2)}) copy-start(bf16[4096,512]{1,0:T(8,128)(2,1)} %param.12) | copy-start | bytes 12582916
  155.8 11.3 %collective-permute-start.10 = (bf16[512,512]{0,1:T(8,128)(2,1)S(1)}, bf16[512,512]{0,1:T(8,128)(2,1)S(1)}, u32[]{:S(2)}, u32[]{:S(2)}) collective-permute-start(bf16[512,512]{0,1:T(8,128)(2,1)S(1)} %collective-permute-done.9), channel_id=1, source_target_pairs={{0,7},{1,0},{2,1},{3,2},{4,3},{5,4},{6,5},{7,6},{8,15},{9,8},{10,9... | collective-permute-start | bytes 1572872 | tf_op jit(solution)/shard_map/ppermute | solution.py:19
  168.5 3.3 %copy-start.1 = (bf16[4096,128]{1,0:T(8,128)(2,1)S(1)}, bf16[4096,128]{1,0:T(8,128)(2,1)}, u32[]{:S(2)}) copy-start(bf16[4096,128]{1,0:T(8,128)(2,1)} %param.11) | copy-start | bytes 3145732
